TPU v7x, 32 devices: a whole 2x2x4 slice. The times are simulated.
32 devices in a mesh: seq: 4 (over y, x), tp: 8 (over z, core).
Axes of the slice: x: 2, y: 2, z: 4, core: 2. Of those that a mesh axis runs over, the one named last changes fastest.
Arguments:
- tokens: bfloat16 [1, 512, 4096], P(None, 'seq', 'tp'), may hold values from -6 to 6
- projections: bfloat16 [4096, 3, 4096], P(None, None, 'tp'), may hold values from -1.5 to 1.5
- out_weight: bfloat16 [4096, 4096], P('tp'), may hold values from -0.09375 to 0.09375
- gain_in: float32 [4096], P('tp'), may hold values from 0.5 to 1.5
- gain_out: float32 [4096], P('tp'), may hold values from 0.5 to 1.5
- iterates: float32 [5, 1, 512, 4096], P(None, None, 'seq', 'tp'), may hold values from -5 to 5
- images: float32 [5, 1, 512, 4096], P(None, None, 'seq', 'tp'), may hold values from -330 to 330
Outputs:
- mixed: float32 [1, 512, 4096], P(None, 'seq', 'tp')
- image: float32 [1, 512, 4096], P(None, 'seq', 'tp')
All inputs are finite; a program needn't handle non-finite values.
Results may differ from a plain program's by a relative error of at most 0.013.
Values may be sent and summed in bfloat16 or wider, within the bound.
No kernel may reach another device: no remote copies, remote signals or barrier semaphores. Data moves between devices by JAX's collectives and lax.ppermute only.
A program may use at most 64 MiB of HBM per device.

v0:
```python
import jax
import jax.numpy as jnp
from jax import lax
from jax.sharding import PartitionSpec as P

HEAD_SIZE = 128
ITERS = 2
epsilon = 1e-05
rope_base = 10000.0
ridge_factor = 0.01


def rotate(vectors, positions):
    half_dim = vectors.shape[-1] // 2
    frequency = rope_base ** (-2.0 * jnp.arange(half_dim).astype(jnp.float32) / vectors.shape[-1])
    angles = positions[:, None] * frequency[None, :]
    cosine = jnp.cos(angles)
    sine_part = jnp.sin(angles)
    first_half = vectors[..., :half_dim]
    second_half = vectors[..., half_dim:]
    return jnp.concatenate(
        [
            first_half * cosine - second_half * sine_part,
            second_half * cosine + first_half * sine_part,
        ],
        axis=-1,
    )


def solve_small(matrix, target):
    extent = matrix.shape[0]
    indices = jnp.arange(extent)
    for column in range(extent):
        factor = jnp.where(indices > column, matrix[:, column] / matrix[column, column], 0.0)
        matrix = matrix - factor[:, None] * matrix[column][None, :]
        target = target - factor * target[column]
    answer = jnp.zeros_like(target)
    for column in reversed(range(extent)):
        entry_value = (target[column] - jnp.sum(matrix[column] * answer)) / matrix[column, column]
        answer = answer.at[column].set(entry_value)
    return answer


def anderson_weights(gram):
    extent = gram.shape[0]
    ridge = ridge_factor * jnp.trace(gram) / extent
    regular = gram + ridge * jnp.eye(extent, dtype=gram.dtype)
    solved = solve_small(regular, jnp.ones((extent,), gram.dtype))
    return solved / jnp.sum(solved)


def pair_products(left, right):
    return jnp.einsum("mbsd,nbsd->mn", left, right, precision=lax.Precision.HIGHEST)


def grow_gram(gram, new_row, own_value):
    upper = jnp.concatenate([gram[1:, 1:], new_row[:, None]], axis=1)
    lower = jnp.concatenate([new_row, own_value[None]])[None, :]
    return jnp.concatenate([upper, lower], axis=0)


def shards(tokens, projections, out_weight, gain_in, gain_out, iterates, images):
    batch_count, local_length, local_width = tokens.shape
    full_width = local_width * lax.axis_size("tp")
    heads = projections.shape[2] // HEAD_SIZE
    seq_start = lax.axis_index("seq") * local_length
    query_index = seq_start + jnp.arange(local_length, dtype=jnp.int32)
    positions = query_index.astype(jnp.float32)
    score_scale = HEAD_SIZE ** (-0.5)
    residuals = images - iterates
    gram = lax.psum(pair_products(residuals, residuals), ("seq", "tp"))
    mixed = iterates[0]
    image = images[0]
    for step_index in range(ITERS):
        alpha = anderson_weights(gram)
        mixed = jnp.einsum("m,mbsd->bsd", alpha, images, precision=lax.Precision.HIGHEST)
        layer_squares = lax.psum(jnp.sum(mixed * mixed, axis=-1), "tp")
        layer_row_scale = lax.rsqrt(layer_squares / full_width + epsilon)
        normed = (mixed * layer_row_scale[..., None] * gain_in).astype(jnp.bfloat16)
        empty = jnp.zeros((batch_count, local_length, 3, projections.shape[2]), jnp.float32)
        piece = lax.all_gather(normed, "tp", axis=2, tiled=True)
        rows = lax.slice_in_dim(projections, 0, piece.shape[2], axis=0)
        mapped = empty + jnp.einsum(
            "bsd,dce->bsce", piece, rows, preferred_element_type=jnp.float32
        )
        pieces = mapped.reshape(batch_count, local_length, 3, heads, HEAD_SIZE).transpose(
            2, 0, 3, 1, 4
        )
        query_rows = rotate(pieces[0], positions).astype(jnp.bfloat16)
        key_rows = rotate(pieces[1], positions).astype(jnp.bfloat16)
        value_rows = pieces[2].astype(jnp.bfloat16)
        row_shape = (batch_count, heads, local_length)
        best = jnp.full(row_shape, -1e30, jnp.float32)
        key_piece = lax.all_gather(key_rows, "seq", axis=2, tiled=True)
        value_piece = lax.all_gather(value_rows, "seq", axis=2, tiled=True)
        logit_scores = (
            jnp.einsum("bhqd,bhkd->bhqk", query_rows, key_piece, preferred_element_type=jnp.float32)
            * score_scale
        )
        key_index = jnp.arange(key_piece.shape[2], dtype=jnp.int32)
        allowed = key_index[None, :] <= query_index[:, None]
        logit_scores = jnp.where(allowed, logit_scores, -1e30)
        newest = jnp.maximum(best, jnp.max(logit_scores, axis=-1))
        softmax_weights = jnp.where(allowed, jnp.exp(logit_scores - newest[..., None]), 0.0)
        total = jnp.sum(softmax_weights, axis=-1)
        accum = jnp.einsum(
            "bhqk,bhkd->bhqd",
            softmax_weights.astype(jnp.bfloat16),
            value_piece,
            preferred_element_type=jnp.float32,
        )
        best, total, accum = (newest, total, accum)
        attended = (
            (accum / total[..., None])
            .astype(jnp.bfloat16)
            .transpose(0, 2, 1, 3)
            .reshape(batch_count, local_length, heads * HEAD_SIZE)
        )
        partial_value = jnp.einsum(
            "bse,ed->bsd", attended, out_weight, preferred_element_type=jnp.float32
        )
        attention = lax.psum_scatter(
            partial_value.astype(jnp.bfloat16), "tp", scatter_dimension=2, tiled=True
        ).astype(jnp.float32)
        layer_summed = tokens.astype(jnp.float32) + attention
        scaled = layer_summed * gain_out
        if step_index + 1 == ITERS:
            finish_squares = lax.psum(jnp.sum(layer_summed * layer_summed, axis=-1), "tp")
            image = scaled * lax.rsqrt(finish_squares / full_width + epsilon)[..., None]
        else:
            advance_gram = gram
            advance_residuals = residuals
            kept = advance_residuals[1:]
            cross_scaled = jnp.einsum(
                "bsd,mbsd->mbs", scaled, kept, precision=lax.Precision.HIGHEST
            )
            cross_mixed = jnp.einsum("bsd,mbsd->mbs", mixed, kept, precision=lax.Precision.HIGHEST)
            totals = lax.psum(
                (
                    jnp.sum(layer_summed * layer_summed, axis=-1),
                    cross_scaled,
                    cross_mixed,
                    jnp.sum(scaled * scaled, axis=-1),
                    jnp.sum(scaled * mixed, axis=-1),
                    jnp.sum(mixed * mixed, axis=-1),
                ),
                "tp",
            )
            squares, scaled_cross, mixed_cross, scaled_own, joint_own, mixed_own = totals
            row_scale = lax.rsqrt(squares / full_width + epsilon)
            advance_image = scaled * row_scale[..., None]
            row_terms = jnp.sum(row_scale[None] * scaled_cross - mixed_cross, axis=(1, 2))
            own_terms = jnp.sum(
                row_scale * row_scale * scaled_own - 2.0 * row_scale * joint_own + mixed_own
            )
            new_row, own_value = lax.psum((row_terms, own_terms), "seq")
            advance_residuals = jnp.concatenate([kept, (advance_image - mixed)[None]], axis=0)
            advance_gram = grow_gram(advance_gram, new_row, own_value)
            image = advance_image
            residuals = advance_residuals
            gram = advance_gram
            images = jnp.concatenate([images[1:], image[None]], axis=0)
    return (mixed, image)


def solution(mesh):
    in_specs = (
        P(None, "seq", "tp"),
        P(None, None, "tp"),
        P("tp", None),
        P("tp"),
        P("tp"),
        P(None, None, "seq", "tp"),
        P(None, None, "seq", "tp"),
    )
    out_specs = (P(None, "seq", "tp"), P(None, "seq", "tp"))
    return jax.shard_map(shards, mesh=mesh, in_specs=in_specs, out_specs=out_specs, check_vma=False)
```

profile of v0, /device:TPU:0, one launch (start us, length us, event | category | flops | bytes accessed | tf_op | source)
XLA Modules:
  0.0 377.3 jit_solution(1337387105630204352)
XLA Ops:
  7.2 2.0 sub.129
  11.3 5.0 %convolution_bitcast_fusion.1 = f32[5,5]{1,0:T(8,128)S(1)} fusion(f32[5,128,512]{1,0,2:T(8,128)S(1)} %copy.29), kind=kOutput, calls=%fused_computation.18 | convolution fusion | flops 19660800 | bytes 1310820 | tf_op jit(solution)/shard_map/mbsd,nbsd->mn/dot_general | solution.py:53
  16.3 42.0 %psum.80 = f32[5,5]{1,0:T(8,128)S(1)} all-reduce(f32[5,5]{1,0:T(8,128)S(1)} %convolution_bitcast_fusion.1), channel_id=1, replica_groups=mesh['seq'=4,'tp'=8] {'seq','tp'}, use_global_device_ids=true, to_apply=%region_0.0 | all-reduce | flops 25 | bytes 200 | tf_op jit(solution)/shard_map/psum | solution.py:71
  86.7 3.2 fusion.4
  90.0 14.4 %psum.81 = f32[1,128]{1,0:T(1,128)S(1)} all-reduce(f32[1,128]{1,0:T(1,128)S(1)} %bitcast.256), channel_id=1, replica_groups=mesh['seq'=4,'tp'=8] {'tp'}, use_global_device_ids=true, to_apply=%region_9.10 | all-reduce | flops 128 | bytes 1024 | tf_op jit(solution)/shard_map/psum | solution.py:77
  105.3 17.0 %copy.54 = bf16[3,512,4096]{2,1,0:T(8,128)(2,1)} copy(bf16[3,512,4096]{1,2,0:T(8,128)(2,1)} %bitcast.243) | data formatting | bytes 25165824 | tf_op jit(solution)/shard_map/bsd,dce->bsce/dot_general | solution.py:83
  122.6 3.1 all-gather.7.cloned.1.call-done
  125.7 6.7 %fusion.11 = f32[128,3,4,128]{0,3,2,1:T(8,128)S(1)} fusion(bf16[3,4,128,4096]{3,2,1,0:T(8,128)(2,1)} %bitcast.240, bf16[128,4096]{1,0:T(8,128)(2,1)} %all-gather.7.cloned.1.call-done), kind=kOutput, calls=%fused_computation.21 | convolution fusion | flops 1610612736 | bytes 14417920 | tf_op jit(solution)/shard_map/bsd,dce->bsce/dot_general | solution.py:83
  132.6 10.0 %all_gather.19 = bf16[1,4,512,128]{2,3,1,0:T(8,128)(2,1)S(1)} all-gather(bf16[1,4,128,128]{2,3,1,0:T(8,128)(2,1)S(1)} %pad_maximum_fusion), channel_id=1, replica_groups=mesh['seq'=4,'tp'=8] {'seq'}, dimensions={2}, use_global_device_ids=true | all-gather | bytes 655360 | tf_op jit(solution)/shard_map/all_gather | solution.py:94
  143.1 11.0 %all-gather.1 = bf16[1,1,4,512,128]{3,4,2,0,1:T(8,128)(2,1)S(1)} all-gather(bf16[1,1,4,128,128]{3,4,2,0,1:T(8,128)(2,1)S(1)} %slice.565), channel_id=3, replica_groups=mesh['seq'=4,'tp'=8] {'seq'}, dimensions={3}, use_global_device_ids=true | all-gather | bytes 655360 | tf_op jit(solution)/shard_map/all_gather | solution.py:95
  159.4 28.7 %reduce-scatter.3.cloned.1.call-done = bf16[1,128,512]{2,1,0:T(8,128)(2,1)} async-done(((bf16[1,128,4096]{2,1,0:T(8,128)(2,1)}), bf16[1,128,512]{2,1,0:T(8,128)(2,1)}) %reduce-scatter.3.cloned.1.call-update) | async-done | bytes 131088 | tf_op jit(solution)/shard_map/reduce_scatter | solution.py:122
  189.2 5.9 %fusion.15 = f32[128,1,4]{2,1,0:T(1,128)S(1)} fusion(f32[4,128,512]{2,1,0:T(8,128)} %slice_bitcast_fusion, f32[128,512,1]{1,0,2:T(8,128)S(1)} %get-tuple-element.164), kind=kOutput, calls=%fused_computation.27 | convolution fusion | flops 3145728 | bytes 1312768 | tf_op jit(solution)/shard_map/bsd,mbsd->mbs/dot_general | solution.py:134
  195.2 4.6 %fusion.13 = f32[128,1,4]{2,1,0:T(1,128)S(1)} fusion(f32[4,128,512]{2,1,0:T(8,128)S(1)} %copy-done.8, f32[128,512,1]{1,0,2:T(8,128)S(1)} %get-tuple-element.165), kind=kOutput, calls=%fused_computation.25 | convolution fusion | flops 3145728 | bytes 1312768 | tf_op jit(solution)/shard_map/bsd,mbsd->mbs/dot_general | solution.py:137
  199.8 13.9 %all-reduce.2 = (f32[1,128]{1,0:T(1,128)S(1)}, f32[1,128]{1,0:T(1,128)S(1)}, f32[1,128]{1,0:T(1,128)S(1)}, f32[4,1,128]{2,0,1:T(4,128)S(1)}, f32[4,1,128]{2,0,1:T(4,128)S(1)}) all-reduce(f32[1,128]{1,0:T(1,128)S(1)} %bitcast.254, f32[1,128]{1,0:T(1,128)S(1)} %bitcast.253, ...), channel_id=1, replica_groups=mesh['seq'=4,'tp'=8] {'tp'}, use_global_device_ids=true, to_apply=%region_14.15 | all-reduce | flops 1408 | bytes 11264 | tf_op jit(solution)/shard_map/psum | solution.py:138
  214.5 11.1 %all-reduce.3 = (f32[1]{0:T(128)}, f32[4]{0:T(128)S(1)}) all-reduce(f32[1]{0:T(128)} %bitcast.72, f32[4]{0:T(128)S(1)} %subtract_reduce_fusion), channel_id=1, replica_groups=mesh['seq'=4,'tp'=8] {'seq'}, use_global_device_ids=true, to_apply=%region_24.25 | all-reduce | flops 5 | bytes 40 | tf_op jit(solution)/shard_map/psum | solution.py:156
  255.6 3.2 fusion.2
  259.0 13.6 %psum.89 = f32[1,128]{1,0:T(1,128)S(1)} all-reduce(f32[1,128]{1,0:T(1,128)S(1)} %bitcast.255), channel_id=1, replica_groups=mesh['seq'=4,'tp'=8] {'tp'}, use_global_device_ids=true, to_apply=%region_33.34 | all-reduce | flops 128 | bytes 1024 | tf_op jit(solution)/shard_map/psum | solution.py:77
  273.4 18.7 %all-gather.9.cloned.1.call-done = bf16[128,4096]{1,0:T(8,128)(2,1)} async-done(((bf16[128,512]{1,0:T(8,128)(2,1)}), bf16[128,4096]{1,0:T(8,128)(2,1)}) %all-gather.9.cloned.1.call-update) | async-done | bytes 1048592 | tf_op jit(solution)/shard_map/all_gather | solution.py:81
  292.1 6.7 %convolution_bitcast_fusion = f32[3,1,4,128,128]{3,4,2,1,0:T(8,128)S(1)} fusion(bf16[3,4,128,4096]{3,2,1,0:T(8,128)(2,1)} %bitcast.241, bf16[128,4096]{1,0:T(8,128)(2,1)} %all-gather.9.cloned.1.call-done), kind=kOutput, calls=%fused_computation.13 | convolution fusion | flops 1610612736 | bytes 14417920 | tf_op jit(solution)/shard_map/bsd,dce->bsce/dot_general | solution.py:83
  299.0 10.0 %all_gather.22 = bf16[1,4,512,128]{2,3,1,0:T(8,128)(2,1)S(1)} all-gather(bf16[1,4,128,128]{2,3,1,0:T(8,128)(2,1)S(1)} %pad_maximum_fusion.1), channel_id=1, replica_groups=mesh['seq'=4,'tp'=8] {'seq'}, dimensions={2}, use_global_device_ids=true | all-gather | bytes 655360 | tf_op jit(solution)/shard_map/all_gather | solution.py:94
  309.5 10.8 %all-gather.3 = bf16[1,1,4,512,128]{3,4,2,1,0:T(8,128)(2,1)S(1)} all-gather(bf16[1,1,4,128,128]{3,4,2,1,0:T(8,128)(2,1)S(1)} %slice.564), channel_id=5, replica_groups=mesh['seq'=4,'tp'=8] {'seq'}, dimensions={3}, use_global_device_ids=true | all-gather | bytes 655360 | tf_op jit(solution)/shard_map/all_gather | solution.py:95
  321.1 1.7 fusion.1
  322.8 31.4 %reduce-scatter.5.cloned.1.call-done = bf16[1,128,512]{2,1,0:T(8,128)(2,1)} async-done(((bf16[1,128,4096]{2,1,0:T(8,128)(2,1)}), bf16[1,128,512]{2,1,0:T(8,128)(2,1)}) %reduce-scatter.5.cloned.1.call-update) | async-done | bytes 131088 | tf_op jit(solution)/shard_map/reduce_scatter | solution.py:122
  355.3 13.8 %psum.90 = f32[1,128]{1,0:T(1,128)S(1)} all-reduce(f32[1,128]{1,0:T(1,128)S(1)} %bitcast.257), channel_id=1, replica_groups=mesh['seq'=4,'tp'=8] {'tp'}, use_global_device_ids=true, to_apply=%region_38.39 | all-reduce | flops 128 | bytes 1024 | tf_op jit(solution)/shard_map/psum | solution.py:128
  (165 shorter events, 53.9 us)
Async XLA Ops:
  7.2 118.5 %all-gather.7.cloned.1.call-start = ((), (), s32[]{:S(2)}) async-start(), calls=%async_computation.4 | async-start | bytes 1179648 | tf_op jit(solution)/shard_map/all_gather | solution.py:81
  9.2 1.1 copy-start.3
  11.3 75.4 %copy-start.2 = (f32[5,1,128,512]{3,2,1,0:T(8,128)S(1)}, f32[5,1,128,512]{3,2,1,0:T(8,128)}, u32[]{:S(2)}) copy-start(f32[5,1,128,512]{3,2,1,0:T(8,128)} %param.33) | copy-start | bytes 3932164
  16.3 88.2 %copy-start.11 = (f32[512]{0:T(512)S(1)}, f32[512]{0:T(512)}, u32[]{:S(2)}) copy-start(f32[512]{0:T(512)} %param.30) | copy-start | bytes 6148
  105.2 82.9 %reduce-scatter.3.cloned.1.call-start = ((), (), s32[]{:S(2)}) async-start(), calls=%async_computation.2 | async-start | bytes 1179648 | tf_op jit(solution)/shard_map/reduce_scatter | solution.py:122
  143.0 11.8 %copy-start = (bf16[512,4096]{1,0:T(8,128)(2,1)S(1)}, bf16[512,4096]{1,0:T(8,128)(2,1)}, u32[]{:S(2)}) copy-start(bf16[512,4096]{1,0:T(8,128)(2,1)} %param.29) | copy-start | bytes 12582916
  156.6 1.7 copy-start.4
  156.6 135.5 %all-gather.9.cloned.1.call-start = ((), (), s32[]{:S(2)}) async-start(), calls=%async_computation.5 | async-start | bytes 1179648 | tf_op jit(solution)/shard_map/all_gather | solution.py:81
  156.7 31.4 %copy-start.6 = (bf16[1,128,512]{2,1,0:T(8,128)(2,1)S(1)}, bf16[1,128,512]{2,1,0:T(8,128)(2,1)}, u32[]{:S(2)}) copy-start(bf16[1,128,512]{2,1,0:T(8,128)(2,1)} %param.27) | copy-start | bytes 393220
  156.7 31.4 %copy-start.10 = (f32[512]{0:T(512)S(1)}, f32[512]{0:T(512)}, u32[]{:S(2)}) copy-start(f32[512]{0:T(512)} %param.31) | copy-start | bytes 6148
  159.4 35.8 %copy-start.8 = (f32[4,128,512]{2,1,0:T(8,128)S(1)}, f32[4,128,512]{2,1,0:T(8,128)}, u32[]{:S(2)}) copy-start(f32[4,128,512]{2,1,0:T(8,128)} %slice_bitcast_fusion) | copy-start | bytes 3145732
  189.2 66.2 %copy-start.9 = (bf16[1,128,512]{2,1,0:T(8,128)(2,1)S(1)}, bf16[1,128,512]{2,1,0:T(8,128)(2,1)}, u32[]{:S(2)}) copy-start(bf16[1,128,512]{2,1,0:T(8,128)(2,1)} %reduce-scatter.3.cloned.1.call-done) | copy-start | bytes 393220
  189.2 66.3 %copy-start.5 = (f32[4,1,128,512]{3,2,1,0:T(8,128)S(1)}, f32[4,1,128,512]{3,2,1,0:T(8,128)}, u32[]{:S(2)}) copy-start(f32[4,1,128,512]{3,2,1,0:T(8,128)} %slice.432) | copy-start | bytes 3145732
  258.9 39.8 %copy-start.7 = (f32[1,128,512]{2,1,0:T(8,128)}, f32[1,128,512]{2,1,0:T(8,128)S(1)}, u32[]{:S(2)}) copy-start(f32[1,128,512]{2,1,0:T(8,128)S(1)} %get-tuple-element.153) | copy-start | bytes 786436
  273.3 80.9 %reduce-scatter.5.cloned.1.call-start = ((), (), s32[]{:S(2)}) async-start(), calls=%async_computation.3 | async-start | bytes 1179648 | tf_op jit(solution)/shard_map/reduce_scatter | solution.py:122
  309.4 11.6 %copy-start.1 = (bf16[512,4096]{1,0:T(8,128)(2,1)S(1)}, bf16[512,4096]{1,0:T(8,128)(2,1)}, u32[]{:S(2)}) copy-start(bf16[512,4096]{1,0:T(8,128)(2,1)} %param.29) | copy-start | bytes 12582916
Sparse Core Ops, SparseCore 0:
  105.4 20.2 all-gather.6
  156.7 31.3 reduce-scatter.2
  273.5 18.5 all-gather.8
  322.9 31.2 reduce-scatter.4
where the time goes:
time: 379 us; the launch traced here: 377 us
  blocking collectives  151 us (40%)
  waiting for transfers between devices  81.9 us (22%)
  matrix products  40.5 us (11%)
  local copies, waits for them, and re-layouts  35.5 us (9%)
  between operations  34.9 us (9%)
  other arithmetic  33.6 us (9%)
    reduce_scatter x2, waiting for transfers between devices, shards(): lax.psum_scatter(partial_value.astype(jnp.bfloat16), 'tp', scatter_dimens...  60.1 us
    psum x1, blocking collectives, shards(): gram = lax.psum(pair_products(residuals, residuals), ('seq', 'tp'))  42 us
    psum x2, blocking collectives, shards(): layer_squares = lax.psum(jnp.sum(mixed * mixed, axis=-1), 'tp')  28 us
    all_gather x2, blocking collectives, shards(): value_piece = lax.all_gather(value_rows, 'seq', axis=2, tiled=True)  21.8 us
    all_gather x2, waiting for transfers between devices, shards(): piece = lax.all_gather(normed, 'tp', axis=2, tiled=True)  21.8 us
    all_gather x2, blocking collectives, shards(): key_piece = lax.all_gather(key_rows, 'seq', axis=2, tiled=True)  20 us
    dot_general x1, local copies, waits for them, and re-layouts, shards(): jnp.einsum('bsd,dce->bsce', piece, rows, preferred_element_type=jnp.float32)  17 us
    psum x1, blocking collectives, shards(): lax.psum((jnp.sum(layer_summed * layer_summed, axis=-1), cross_scaled, cr...  13.9 us
  transfers between devices with their start and end apart: 4, of which 4 were waited for; matrix products, arithmetic and copies ran while one was open for 5% of the time, Pallas kernels for 0%

commit v1 on v0

--- a/solution.py
+++ b/solution.py
@@ -68,7 +68,7 @@
     positions = query_index.astype(jnp.float32)
     score_scale = HEAD_SIZE ** (-0.5)
     residuals = images - iterates
-    gram = lax.psum(pair_products(residuals, residuals), ("seq", "tp"))
+    gram = lax.psum(lax.psum(pair_products(residuals, residuals), "tp"), "seq")
     mixed = iterates[0]
     image = images[0]
     for step_index in range(ITERS):

time: 379 us -> 362 us (0.955)
  blocking collectives: 151 us -> 136 us
    psum x1 -> x2, blocking collectives: 42 us -> 28.1 us  [shards(): gram = lax.psum(lax.psum(pair_products(residuals, residuals), 'tp'), 'seq')]
where the time goes in v1:
time: 362 us; the launch traced here: 361 us
  blocking collectives  136 us (38%)
  waiting for transfers between devices  80.1 us (22%)
  matrix products  40.5 us (11%)
  local copies, waits for them, and re-layouts  35.5 us (10%)
  between operations  34.9 us (10%)
  other arithmetic  33.6 us (9%)
    reduce_scatter x2, waiting for transfers between devices, shards(): lax.psum_scatter(partial_value.astype(jnp.bfloat16), 'tp', scatter_dimens...  60 us
    psum x2, blocking collectives, shards(): gram = lax.psum(lax.psum(pair_products(residuals, residuals), 'tp'), 'seq')  28.1 us
    psum x2, blocking collectives, shards(): layer_squares = lax.psum(jnp.sum(mixed * mixed, axis=-1), 'tp')  27.2 us
    all_gather x2, blocking collectives, shards(): value_piece = lax.all_gather(value_rows, 'seq', axis=2, tiled=True)  21.8 us
    all_gather x2, waiting for transfers between devices, shards(): piece = lax.all_gather(normed, 'tp', axis=2, tiled=True)  20.1 us
    all_gather x2, blocking collectives, shards(): key_piece = lax.all_gather(key_rows, 'seq', axis=2, tiled=True)  20 us
    dot_general x1, local copies, waits for them, and re-layouts, shards(): jnp.einsum('bsd,dce->bsce', piece, rows, preferred_element_type=jnp.float32)  17 us
    psum x1, blocking collectives, shards(): lax.psum((jnp.sum(layer_summed * layer_summed, axis=-1), cross_scaled, cr...  14.1 us
  transfers between devices with their start and end apart: 4, of which 4 were waited for; matrix products, arithmetic and copies ran while one was open for 5% of the time, Pallas kernels for 0%

profile of v1, /device:TPU:0, one launch (start us, length us, event | category | flops | bytes accessed | tf_op | source)
XLA Modules:
  0.0 361.0 jit_solution(4377590714567800945)
XLA Ops:
  7.2 2.0 sub.129
  11.3 5.0 %convolution_bitcast_fusion.1 = f32[5,5]{1,0:T(8,128)S(1)} fusion(f32[5,128,512]{1,0,2:T(8,128)S(1)} %copy.29), kind=kOutput, calls=%fused_computation.18 | convolution fusion | flops 19660800 | bytes 1310820 | tf_op jit(solution)/shard_map/mbsd,nbsd->mn/dot_general | solution.py:53
  16.3 18.2 %psum.87 = f32[5,5]{1,0:T(8,128)S(1)} all-reduce(f32[5,5]{1,0:T(8,128)S(1)} %convolution_bitcast_fusion.1), channel_id=1, replica_groups=mesh['seq'=4,'tp'=8] {'tp'}, use_global_device_ids=true, to_apply=%region_0.0 | all-reduce | flops 25 | bytes 200 | tf_op jit(solution)/shard_map/psum | solution.py:71
  34.5 9.9 %psum.88 = f32[5,5]{1,0:T(8,128)S(1)} all-reduce(f32[5,5]{1,0:T(8,128)S(1)} %psum.87), channel_id=1, replica_groups=mesh['seq'=4,'tp'=8] {'seq'}, use_global_device_ids=true, to_apply=%region_1.0 | all-reduce | flops 25 | bytes 200 | tf_op jit(solution)/shard_map/psum | solution.py:71
  72.9 3.2 fusion.4
  76.2 13.6 %psum.89 = f32[1,128]{1,0:T(1,128)S(1)} all-reduce(f32[1,128]{1,0:T(1,128)S(1)} %bitcast.256), channel_id=1, replica_groups=mesh['seq'=4,'tp'=8] {'tp'}, use_global_device_ids=true, to_apply=%region_10.11 | all-reduce | flops 128 | bytes 1024 | tf_op jit(solution)/shard_map/psum | solution.py:77
  90.7 17.0 %copy.54 = bf16[3,512,4096]{2,1,0:T(8,128)(2,1)} copy(bf16[3,512,4096]{1,2,0:T(8,128)(2,1)} %bitcast.243) | data formatting | bytes 25165824 | tf_op jit(solution)/shard_map/bsd,dce->bsce/dot_general | solution.py:83
  109.3 6.7 %fusion.11 = f32[128,3,4,128]{0,3,2,1:T(8,128)S(1)} fusion(bf16[3,4,128,4096]{3,2,1,0:T(8,128)(2,1)} %bitcast.240, bf16[128,4096]{1,0:T(8,128)(2,1)} %all-gather.7.cloned.1.call-done), kind=kOutput, calls=%fused_computation.21 | convolution fusion | flops 1610612736 | bytes 14417920 | tf_op jit(solution)/shard_map/bsd,dce->bsce/dot_general | solution.py:83
  116.2 10.0 %all_gather.19 = bf16[1,4,512,128]{2,3,1,0:T(8,128)(2,1)S(1)} all-gather(bf16[1,4,128,128]{2,3,1,0:T(8,128)(2,1)S(1)} %pad_maximum_fusion), channel_id=1, replica_groups=mesh['seq'=4,'tp'=8] {'seq'}, dimensions={2}, use_global_device_ids=true | all-gather | bytes 655360 | tf_op jit(solution)/shard_map/all_gather | solution.py:94
  126.7 11.0 %all-gather.1 = bf16[1,1,4,512,128]{3,4,2,0,1:T(8,128)(2,1)S(1)} all-gather(bf16[1,1,4,128,128]{3,4,2,0,1:T(8,128)(2,1)S(1)} %slice.565), channel_id=3, replica_groups=mesh['seq'=4,'tp'=8] {'seq'}, dimensions={3}, use_global_device_ids=true | all-gather | bytes 655360 | tf_op jit(solution)/shard_map/all_gather | solution.py:95
  143.0 28.6 %reduce-scatter.3.cloned.1.call-done = bf16[1,128,512]{2,1,0:T(8,128)(2,1)} async-done(((bf16[1,128,4096]{2,1,0:T(8,128)(2,1)}), bf16[1,128,512]{2,1,0:T(8,128)(2,1)}) %reduce-scatter.3.cloned.1.call-update) | async-done | bytes 131088 | tf_op jit(solution)/shard_map/reduce_scatter | solution.py:122
  172.8 5.9 %fusion.15 = f32[128,1,4]{2,1,0:T(1,128)S(1)} fusion(f32[4,128,512]{2,1,0:T(8,128)} %slice_bitcast_fusion, f32[128,512,1]{1,0,2:T(8,128)S(1)} %get-tuple-element.164), kind=kOutput, calls=%fused_computation.27 | convolution fusion | flops 3145728 | bytes 1312768 | tf_op jit(solution)/shard_map/bsd,mbsd->mbs/dot_general | solution.py:134
  178.7 4.6 %fusion.13 = f32[128,1,4]{2,1,0:T(1,128)S(1)} fusion(f32[4,128,512]{2,1,0:T(8,128)S(1)} %copy-done.8, f32[128,512,1]{1,0,2:T(8,128)S(1)} %get-tuple-element.165), kind=kOutput, calls=%fused_computation.25 | convolution fusion | flops 3145728 | bytes 1312768 | tf_op jit(solution)/shard_map/bsd,mbsd->mbs/dot_general | solution.py:137
  183.4 14.1 %all-reduce.2 = (f32[1,128]{1,0:T(1,128)S(1)}, f32[1,128]{1,0:T(1,128)S(1)}, f32[1,128]{1,0:T(1,128)S(1)}, f32[4,1,128]{2,0,1:T(4,128)S(1)}, f32[4,1,128]{2,0,1:T(4,128)S(1)}) all-reduce(f32[1,128]{1,0:T(1,128)S(1)} %bitcast.254, f32[1,128]{1,0:T(1,128)S(1)} %bitcast.253, ...), channel_id=1, replica_groups=mesh['seq'=4,'tp'=8] {'tp'}, use_global_device_ids=true, to_apply=%region_15.16 | all-reduce | flops 1408 | bytes 11264 | tf_op jit(solution)/shard_map/psum | solution.py:138
  198.2 11.0 %all-reduce.3 = (f32[1]{0:T(128)}, f32[4]{0:T(128)S(1)}) all-reduce(f32[1]{0:T(128)} %bitcast.72, f32[4]{0:T(128)S(1)} %subtract_reduce_fusion), channel_id=1, replica_groups=mesh['seq'=4,'tp'=8] {'seq'}, use_global_device_ids=true, to_apply=%region_25.26 | all-reduce | flops 5 | bytes 40 | tf_op jit(solution)/shard_map/psum | solution.py:156
  239.3 3.2 fusion.2
  242.6 13.6 %psum.97 = f32[1,128]{1,0:T(1,128)S(1)} all-reduce(f32[1,128]{1,0:T(1,128)S(1)} %bitcast.255), channel_id=1, replica_groups=mesh['seq'=4,'tp'=8] {'tp'}, use_global_device_ids=true, to_apply=%region_34.35 | all-reduce | flops 128 | bytes 1024 | tf_op jit(solution)/shard_map/psum | solution.py:77
  257.0 18.7 %all-gather.9.cloned.1.call-done = bf16[128,4096]{1,0:T(8,128)(2,1)} async-done(((bf16[128,512]{1,0:T(8,128)(2,1)}), bf16[128,4096]{1,0:T(8,128)(2,1)}) %all-gather.9.cloned.1.call-update) | async-done | bytes 1048592 | tf_op jit(solution)/shard_map/all_gather | solution.py:81
  275.7 6.7 %convolution_bitcast_fusion = f32[3,1,4,128,128]{3,4,2,1,0:T(8,128)S(1)} fusion(bf16[3,4,128,4096]{3,2,1,0:T(8,128)(2,1)} %bitcast.241, bf16[128,4096]{1,0:T(8,128)(2,1)} %all-gather.9.cloned.1.call-done), kind=kOutput, calls=%fused_computation.13 | convolution fusion | flops 1610612736 | bytes 14417920 | tf_op jit(solution)/shard_map/bsd,dce->bsce/dot_general | solution.py:83
  282.6 10.0 %all_gather.22 = bf16[1,4,512,128]{2,3,1,0:T(8,128)(2,1)S(1)} all-gather(bf16[1,4,128,128]{2,3,1,0:T(8,128)(2,1)S(1)} %pad_maximum_fusion.1), channel_id=1, replica_groups=mesh['seq'=4,'tp'=8] {'seq'}, dimensions={2}, use_global_device_ids=true | all-gather | bytes 655360 | tf_op jit(solution)/shard_map/all_gather | solution.py:94
  293.1 10.8 %all-gather.3 = bf16[1,1,4,512,128]{3,4,2,1,0:T(8,128)(2,1)S(1)} all-gather(bf16[1,1,4,128,128]{3,4,2,1,0:T(8,128)(2,1)S(1)} %slice.564), channel_id=5, replica_groups=mesh['seq'=4,'tp'=8] {'seq'}, dimensions={3}, use_global_device_ids=true | all-gather | bytes 655360 | tf_op jit(solution)/shard_map/all_gather | solution.py:95
  304.7 1.7 fusion.1
  306.5 31.4 %reduce-scatter.5.cloned.1.call-done = bf16[1,128,512]{2,1,0:T(8,128)(2,1)} async-done(((bf16[1,128,4096]{2,1,0:T(8,128)(2,1)}), bf16[1,128,512]{2,1,0:T(8,128)(2,1)}) %reduce-scatter.5.cloned.1.call-update) | async-done | bytes 131088 | tf_op jit(solution)/shard_map/reduce_scatter | solution.py:122
  338.9 13.8 %psum.98 = f32[1,128]{1,0:T(1,128)S(1)} all-reduce(f32[1,128]{1,0:T(1,128)S(1)} %bitcast.257), channel_id=1, replica_groups=mesh['seq'=4,'tp'=8] {'tp'}, use_global_device_ids=true, to_apply=%region_39.40 | all-reduce | flops 128 | bytes 1024 | tf_op jit(solution)/shard_map/psum | solution.py:128
  (166 shorter events, 55.3 us)
Async XLA Ops:
  7.2 102.2 %all-gather.7.cloned.1.call-start = ((), (), s32[]{:S(2)}) async-start(), calls=%async_computation.4 | async-start | bytes 1179648 | tf_op jit(solution)/shard_map/all_gather | solution.py:81
  9.2 1.1 copy-start.3
  11.3 61.6 %copy-start.2 = (f32[5,1,128,512]{3,2,1,0:T(8,128)S(1)}, f32[5,1,128,512]{3,2,1,0:T(8,128)}, u32[]{:S(2)}) copy-start(f32[5,1,128,512]{3,2,1,0:T(8,128)} %param.33) | copy-start | bytes 3932164
  16.3 73.5 %copy-start.11 = (f32[512]{0:T(512)S(1)}, f32[512]{0:T(512)}, u32[]{:S(2)}) copy-start(f32[512]{0:T(512)} %param.30) | copy-start | bytes 6148
  90.6 81.0 %reduce-scatter.3.cloned.1.call-start = ((), (), s32[]{:S(2)}) async-start(), calls=%async_computation.2 | async-start | bytes 1179648 | tf_op jit(solution)/shard_map/reduce_scatter | solution.py:122
  126.7 11.8 %copy-start = (bf16[512,4096]{1,0:T(8,128)(2,1)S(1)}, bf16[512,4096]{1,0:T(8,128)(2,1)}, u32[]{:S(2)}) copy-start(bf16[512,4096]{1,0:T(8,128)(2,1)} %param.29) | copy-start | bytes 12582916
  140.2 1.7 copy-start.4
  140.3 135.5 %all-gather.9.cloned.1.call-start = ((), (), s32[]{:S(2)}) async-start(), calls=%async_computation.5 | async-start | bytes 1179648 | tf_op jit(solution)/shard_map/all_gather | solution.py:81
  140.4 31.3 %copy-start.6 = (bf16[1,128,512]{2,1,0:T(8,128)(2,1)S(1)}, bf16[1,128,512]{2,1,0:T(8,128)(2,1)}, u32[]{:S(2)}) copy-start(bf16[1,128,512]{2,1,0:T(8,128)(2,1)} %param.27) | copy-start | bytes 393220
  140.4 31.3 %copy-start.10 = (f32[512]{0:T(512)S(1)}, f32[512]{0:T(512)}, u32[]{:S(2)}) copy-start(f32[512]{0:T(512)} %param.31) | copy-start | bytes 6148
  143.0 35.7 %copy-start.8 = (f32[4,128,512]{2,1,0:T(8,128)S(1)}, f32[4,128,512]{2,1,0:T(8,128)}, u32[]{:S(2)}) copy-start(f32[4,128,512]{2,1,0:T(8,128)} %slice_bitcast_fusion) | copy-start | bytes 3145732
  172.7 66.3 %copy-start.9 = (bf16[1,128,512]{2,1,0:T(8,128)(2,1)S(1)}, bf16[1,128,512]{2,1,0:T(8,128)(2,1)}, u32[]{:S(2)}) copy-start(bf16[1,128,512]{2,1,0:T(8,128)(2,1)} %reduce-scatter.3.cloned.1.call-done) | copy-start | bytes 393220
  172.7 66.4 %copy-start.5 = (f32[4,1,128,512]{3,2,1,0:T(8,128)S(1)}, f32[4,1,128,512]{3,2,1,0:T(8,128)}, u32[]{:S(2)}) copy-start(f32[4,1,128,512]{3,2,1,0:T(8,128)} %slice.432) | copy-start | bytes 3145732
  242.6 39.9 %copy-start.7 = (f32[1,128,512]{2,1,0:T(8,128)}, f32[1,128,512]{2,1,0:T(8,128)S(1)}, u32[]{:S(2)}) copy-start(f32[1,128,512]{2,1,0:T(8,128)S(1)} %get-tuple-element.153) | copy-start | bytes 786436
  257.0 80.9 %reduce-scatter.5.cloned.1.call-start = ((), (), s32[]{:S(2)}) async-start(), calls=%async_computation.3 | async-start | bytes 1179648 | tf_op jit(solution)/shard_map/reduce_scatter | solution.py:122
  293.1 11.6 %copy-start.1 = (bf16[512,4096]{1,0:T(8,128)(2,1)S(1)}, bf16[512,4096]{1,0:T(8,128)(2,1)}, u32[]{:S(2)}) copy-start(bf16[512,4096]{1,0:T(8,128)(2,1)} %param.29) | copy-start | bytes 12582916
Sparse Core Ops, SparseCore 0:
  90.7 18.5 all-gather.6
  140.4 31.2 reduce-scatter.2
  257.1 18.5 all-gather.8
  306.6 31.2 reduce-scatter.4
